TPU v7x, 32 devices: a whole 2x2x4 slice. The times are simulated.
32 devices in a mesh: vessel: 2 (over core), gather: 16 (over z, y, x).
Axes of the slice: x: 2, y: 2, z: 4, core: 2. Of those that a mesh axis runs over, the one named last changes fastest.
Arguments:
- observed: bfloat16 [16, 16, 2048], P('gather'), may hold values from -6 to 6
- estimate: bfloat16 [2, 16, 16, 2048], P('vessel', 'gather'), may hold values from -6 to 6
- delays: int32 [2, 16], P('vessel', 'gather'), may hold values from 0 to 256
- taps_time: float32 [16, 7], replicated, may hold values from -2 to 2
- taps_shot: float32 [16, 7], replicated, may hold values from -0.5 to 0.5
- thresh: float32 [16], replicated, may hold values from 0.02 to 0.3
Outputs:
- deblended: bfloat16 [2, 16, 16, 2048], P('vessel', 'gather')
All inputs are finite; a program needn't handle non-finite values.
Results may differ from a plain program's by a relative error of at most 0.022.
Values may be sent and summed in bfloat16 or wider, within the bound.
A program may use at most 64 MiB of HBM per device.

v0:
```python
import jax
import jax.numpy as jnp
from jax import lax
from jax.sharding import PartitionSpec as P

TIME_SPACING = 4
SHOT_SPACING = 2
MAXD = 256
ITERS = 2


def late_shift(traces, shift_by):
    width = traces.shape[2]
    padded = jnp.pad(traces, ((0, 0), (0, 0), (MAXD, MAXD)))

    def late_single(trace, shift_amount):
        return lax.dynamic_slice_in_dim(trace, MAXD - shift_amount, width, 1)

    return jax.vmap(late_single)(padded, shift_by)


def early_shift(traces, shift_by):
    width = traces.shape[2]
    padded = jnp.pad(traces, ((0, 0), (0, 0), (MAXD, MAXD)))

    def early_single(trace, shift_amount):
        return lax.dynamic_slice_in_dim(trace, MAXD + shift_amount, width, 1)

    return jax.vmap(early_single)(padded, shift_by)


def along_time(field, taps, shift_sign):
    filter_reach = 3 * TIME_SPACING
    length = field.shape[3]
    padded = jnp.pad(field, ((0, 0), (0, 0), (0, 0), (filter_reach, filter_reach)))
    total = jnp.zeros((taps.shape[0],) + field.shape[1:], jnp.float32)
    for tap_index in range(-3, 4):
        start_offset = filter_reach + shift_sign * tap_index * TIME_SPACING
        total = (
            total
            + taps[:, tap_index + 3][:, None, None, None]
            * padded[:, :, :, start_offset : start_offset + length]
        )
    return total


def along_shots(field, taps, shift_sign):
    filter_reach = 3 * SHOT_SPACING
    length = field.shape[1]
    padded = jnp.pad(field, ((0, 0), (filter_reach, filter_reach), (0, 0), (0, 0)))
    total = jnp.zeros((taps.shape[0],) + field.shape[1:], jnp.float32)
    for tap_index in range(-3, 4):
        start_offset = filter_reach + shift_sign * tap_index * SHOT_SPACING
        total = (
            total
            + taps[:, tap_index + 3][:, None, None, None]
            * padded[:, start_offset : start_offset + length]
        )
    return total


def shrink_filter(plane, taps_time, taps_shot, thresh):
    field = plane.astype(jnp.float32)[None]
    group_time = taps_time.reshape(-1, 4, taps_time.shape[1])
    group_shot = taps_shot.reshape(-1, 4, taps_shot.shape[1])
    group_thresh = thresh.reshape(-1, 4)

    def channel(carry, pieces):
        time_taps, shot_taps, limits = pieces
        forward_pass = along_shots(along_time(field, time_taps, 1), shot_taps, 1)
        bound = limits[:, None, None, None]
        shrunk = forward_pass - jnp.clip(forward_pass, -bound, bound)
        back = along_time(along_shots(shrunk, shot_taps, -1), time_taps, -1)
        return (carry + jnp.sum(back, axis=0), None)

    total, _ = lax.scan(
        channel, jnp.zeros(plane.shape, jnp.float32), (group_time, group_shot, group_thresh)
    )
    return total.astype(jnp.bfloat16)


def pseudo_planes(current, observed, shot_delays):
    own = late_shift(current[0], shot_delays[0])
    blend = lax.psum(own, "vessel").astype(jnp.float32)
    resid = observed.astype(jnp.float32) - blend
    plane = current[0].astype(jnp.float32) + early_shift(resid, shot_delays[0])
    return plane.astype(jnp.bfloat16)[None]


def per_device(observed, estimate, delays, taps_time, taps_shot, thresh):
    current = estimate
    for step in range(ITERS):
        planes = pseudo_planes(current, observed, delays)
        filtered = jnp.stack(
            [
                shrink_filter(
                    lax.all_to_all(planes, "gather", split_axis=2, concat_axis=1, tiled=True)[0],
                    taps_time,
                    taps_shot,
                    thresh,
                )
            ]
        )
        current = lax.all_to_all(filtered, "gather", split_axis=1, concat_axis=2, tiled=True)
    return current


def solution(mesh):
    return jax.shard_map(
        per_device,
        mesh=mesh,
        in_specs=(
            P("gather", None, None),
            P("vessel", "gather", None, None),
            P("vessel", "gather"),
            P(),
            P(),
            P(),
        ),
        out_specs=P("vessel", "gather", None, None),
        check_vma=False,
    )
```

profile of v0, /device:TPU:0, one launch (start us, length us, event | category | flops | bytes accessed | tf_op | source)
XLA Modules:
  0.0 136.3 jit_solution(2640347895954889670)
XLA Ops:
  7.2 1.6 %pad_dynamic-slice_fusion.3 = bf16[1,16,2048]{2,1,0:T(8,128)(2,1)} fusion(s32[]{:T(128)} %bitcast.5, bf16[1,16,2048]{2,1,0:T(8,128)(2,1)} %bitcast.111), kind=kLoop, calls=%fused_computation.150 | loop fusion | bytes 131076 | tf_op jit(solution)/shard_map/vmap()/gather | solution.py:17
  8.8 21.3 %all-reduce.15.cloned.1.call-done = bf16[1,16,2048]{2,1,0:T(8,128)(2,1)} async-done(((bf16[1,16,2048]{2,1,0:T(8,128)(2,1)}), bf16[1,16,2048]{2,1,0:T(8,128)(2,1)}) %all-reduce.15.cloned.1.call-update) | async-done | bytes 65552 | tf_op jit(solution)/shard_map/psum | solution.py:84
  30.1 0.9 convert_subtract_fusion.1
  31.1 0.7 copy-done
  31.9 0.5 broadcast.734
  32.5 1.0 reduce.64
  33.5 0.7 reshape.633
  34.1 7.0 %all-to-all-start = ((bf16[16,2,1024]{2,1,0:T(2,128)(2,1)}), bf16[16,2,1024]{2,1,0:T(2,128)(2,1)S(1)}, u32[]{:S(2)}, u32[]{:S(2)}) async-start(bf16[16,2,1024]{2,1,0:T(2,128)(2,1)} %reshape.633), calls=%async_computation | async-start | bytes 131072 | tf_op jit(solution)/shard_map/all_to_all | solution.py:97
  41.2 0.6 copy-done.3
  41.9 0.6 copy-done.4
  42.6 6.0 %all-to-all-done = bf16[16,2,1024]{2,1,0:T(2,128)(2,1)S(1)} async-done(((bf16[16,2,1024]{2,1,0:T(2,128)(2,1)}), bf16[16,2,1024]{2,1,0:T(2,128)(2,1)S(1)}, u32[]{:S(2)}, u32[]{:S(2)}) %all-to-all-start) | async-done | bytes 65568 | tf_op jit(solution)/shard_map/all_to_all | solution.py:97
  48.9 12.3 %while.30 = (s32[]{:T(128)}, f32[16,1,2048]{2,0,1:T(8,128)S(1)}, f32[4,4,7]{2,1,0:T(4,128)S(1)}, f32[4,4,7]{2,1,0:T(4,128)S(1)}, f32[1,16,1,2048]{3,1,2,0:T(8,12...) while((s32[]{:T(128)}, f32[16,1,2048]{2,0,1:T(8,128)S(1)}, f32[4,4,7]{2,1,0:T(4,128)S(1)}, ...), condition=%wide.region_3.4_spmd.clone, body=%wide.region_1.3_spmd.clone.sunk | while | flops 7372807 | bytes 5506551 | solution.py:76
  49.2 0.3 slice_bitcast_fusion.14
  49.4 0.3 multiply_add_fusion.4
  50.0 0.5 minimum_subtract_fusion.4
  50.5 0.4 fusion.70
  51.0 0.9 add_reduce_fusion.4
  52.2 0.3 slice_bitcast_fusion.14
  52.5 0.3 multiply_add_fusion.4
  53.1 0.5 minimum_subtract_fusion.4
  53.6 0.4 fusion.70
  54.0 0.9 add_reduce_fusion.4
  55.3 0.3 slice_bitcast_fusion.14
  55.6 0.3 multiply_add_fusion.4
  56.1 0.5 minimum_subtract_fusion.4
  56.6 0.4 fusion.70
  57.1 0.9 add_reduce_fusion.4
  58.3 0.3 slice_bitcast_fusion.14
  58.6 0.3 multiply_add_fusion.4
  59.2 0.5 minimum_subtract_fusion.4
  59.7 0.4 fusion.70
  60.2 0.9 add_reduce_fusion.4
  61.2 1.0 reduce.65
  62.2 10.1 %all_to_all.19 = bf16[16,2,1024]{2,1,0:T(2,128)(2,1)S(1)} all-to-all(bf16[16,2,1024]{2,1,0:T(2,128)(2,1)S(1)} %reshape.635), channel_id=1, replica_groups=mesh['vessel'=2,'gather'=16] {'gather'}, dimensions={0} | all-to-all | bytes 131072 | tf_op jit(solution)/shard_map/all_to_all | solution.py:104
  72.5 0.7 pad_dynamic-slice_fusion.2
  73.2 14.6 %all-reduce.17.cloned.1.call-done = bf16[1,16,2048]{2,1,0:T(8,128)(2,1)} async-done(((bf16[1,16,2048]{2,1,0:T(8,128)(2,1)}), bf16[1,16,2048]{2,1,0:T(8,128)(2,1)}) %all-reduce.17.cloned.1.call-update) | async-done | bytes 65552 | tf_op jit(solution)/shard_map/psum | solution.py:84
  87.8 0.9 convert_subtract_fusion
  89.0 1.0 reduce.66
  89.9 0.7 reshape.637
  90.6 6.8 %all-to-all-start.2 = ((bf16[16,2,1024]{2,1,0:T(2,128)(2,1)}), bf16[16,2,1024]{2,1,0:T(2,128)(2,1)S(1)}, u32[]{:S(2)}, u32[]{:S(2)}) async-start(bf16[16,2,1024]{2,1,0:T(2,128)(2,1)} %reshape.637), calls=%async_computation.2 | async-start | bytes 131072 | tf_op jit(solution)/shard_map/all_to_all | solution.py:97
  97.4 7.5 %all-to-all-done.2 = bf16[16,2,1024]{2,1,0:T(2,128)(2,1)S(1)} async-done(((bf16[16,2,1024]{2,1,0:T(2,128)(2,1)}), bf16[16,2,1024]{2,1,0:T(2,128)(2,1)S(1)}, u32[]{:S(2)}, u32[]{:S(2)}) %all-to-all-start.2) | async-done | bytes 65568 | tf_op jit(solution)/shard_map/all_to_all | solution.py:97
  105.2 12.3 %while.31 = (s32[]{:T(128)}, f32[16,1,2048]{2,0,1:T(8,128)S(1)}, f32[4,4,7]{2,1,0:T(4,128)S(1)}, f32[4,4,7]{2,1,0:T(4,128)S(1)}, f32[1,16,1,2048]{3,1,2,0:T(8,12...) while((s32[]{:T(128)}, f32[16,1,2048]{2,0,1:T(8,128)S(1)}, f32[4,4,7]{2,1,0:T(4,128)S(1)}, ...), condition=%wide.region_7.8_spmd.clone, body=%wide.region_5.7_spmd.clone.sunk | while | flops 7372807 | bytes 5506551 | solution.py:76
  105.5 0.3 slice_bitcast_fusion.15
  105.8 0.3 multiply_add_fusion.5
  106.3 0.5 minimum_subtract_fusion.5
  106.9 0.4 fusion.72
  107.3 0.9 add_reduce_fusion.5
  108.6 0.3 slice_bitcast_fusion.15
  108.8 0.3 multiply_add_fusion.5
  109.4 0.5 minimum_subtract_fusion.5
  109.9 0.4 fusion.72
  110.4 0.9 add_reduce_fusion.5
  111.6 0.3 slice_bitcast_fusion.15
  111.9 0.3 multiply_add_fusion.5
  112.5 0.5 minimum_subtract_fusion.5
  113.0 0.4 fusion.72
  113.4 0.9 add_reduce_fusion.5
  115.0 0.3 multiply_add_fusion.5
  115.5 0.5 minimum_subtract_fusion.5
  116.1 0.4 fusion.72
  116.5 0.9 add_reduce_fusion.5
  117.6 1.0 reduce.67
  118.6 10.1 %all_to_all.40 = bf16[16,2,1024]{2,1,0:T(2,128)(2,1)S(1)} all-to-all(bf16[16,2,1024]{2,1,0:T(2,128)(2,1)S(1)} %reshape.639), channel_id=1, replica_groups=mesh['vessel'=2,'gather'=16] {'gather'}, dimensions={0} | all-to-all | bytes 131072 | tf_op jit(solution)/shard_map/all_to_all | solution.py:104
  128.8 0.7 copy.50
  (76 shorter events, 6.5 us)
Async XLA Ops:
  6.5 23.6 %all-reduce.15.cloned.1.call-start = ((), (), s32[]{:S(2)}) async-start(), calls=%async_computation.4 | async-start | bytes 131072 | tf_op jit(solution)/shard_map/psum | solution.py:84
  8.8 21.3 %copy-start.1 = (bf16[1,16,2048]{2,1,0:T(8,128)(2,1)S(1)}, bf16[1,16,2048]{2,1,0:T(8,128)(2,1)}, u32[]{:S(2)}) copy-start(bf16[1,16,2048]{2,1,0:T(8,128)(2,1)} %param.10) | copy-start | bytes 196612
  31.0 0.8 copy-start
  34.1 7.0 %copy-start.2 = (f32[16,7]{0,1:T(8,128)S(1)}, f32[16,7]{0,1:T(8,128)}, u32[]{:S(2)}) copy-start(f32[16,7]{0,1:T(8,128)} %param.13) | copy-start | bytes 1348
  34.1 14.5 %all-to-all-start = ((bf16[16,2,1024]{2,1,0:T(2,128)(2,1)}), bf16[16,2,1024]{2,1,0:T(2,128)(2,1)S(1)}, u32[]{:S(2)}, u32[]{:S(2)}) async-start(bf16[16,2,1024]{2,1,0:T(2,128)(2,1)} %reshape.633), calls=%async_computation | async-start | bytes 131072 | tf_op jit(solution)/shard_map/all_to_all | solution.py:97
  41.1 46.7 %all-reduce.17.cloned.1.call-start = ((), (), s32[]{:S(2)}) async-start(), calls=%async_computation.5 | async-start | bytes 131072 | tf_op jit(solution)/shard_map/psum | solution.py:84
  41.2 0.7 copy-start.3
  41.8 0.7 copy-start.4
  90.6 14.4 %all-to-all-start.2 = ((bf16[16,2,1024]{2,1,0:T(2,128)(2,1)}), bf16[16,2,1024]{2,1,0:T(2,128)(2,1)S(1)}, u32[]{:S(2)}, u32[]{:S(2)}) async-start(bf16[16,2,1024]{2,1,0:T(2,128)(2,1)} %reshape.637), calls=%async_computation.2 | async-start | bytes 131072 | tf_op jit(solution)/shard_map/all_to_all | solution.py:97
Sparse Core Ops, SparseCore 0:
  9.6 20.4 all-reduce.14
  73.3 14.4 all-reduce.16
where the time goes:
time: 137 us; the launch traced here: 136 us
  waiting for transfers between devices  49.5 us (36%)
  other arithmetic  23.8 us (17%)
  blocking collectives  20.2 us (15%)
  between operations  14.3 us (10%)
  local copies, waits for them, and re-layouts  14.1 us (10%)
  starting transfers between devices  13.8 us (10%)
    psum x2, waiting for transfers between devices, pseudo_planes(): blend = lax.psum(own, 'vessel').astype(jnp.float32)  35.9 us
    all_to_all x2, blocking collectives, per_device(): lax.all_to_all(filtered, 'gather', split_axis=1, concat_axis=2, tiled=True)  20.2 us
    all_to_all x2, starting transfers between devices, per_device(): lax.all_to_all(planes, 'gather', split_axis=2, concat_axis=1, tiled=True)[0]  13.8 us
    all_to_all x2, waiting for transfers between devices, per_device(): lax.all_to_all(planes, 'gather', split_axis=2, concat_axis=1, tiled=True)[0]  13.6 us
    reduce_sum x8, other arithmetic, channel(): return (carry + jnp.sum(back, axis=0), None)  7.3 us
    unnamed x26, local copies, waits for them, and re-layouts  5.08 us
    unnamed x8, other arithmetic  4.17 us
    sub x8, other arithmetic, channel(): shrunk = forward_pass - jnp.clip(forward_pass, -bound, bound)  4.06 us
  transfers between devices with their start and end apart: 4, of which 4 were waited for; matrix products, arithmetic and copies ran while one was open for 0% of the time, Pallas kernels for 0%

commit v1 on v0

--- a/solution.py
+++ b/solution.py
@@ -2,6 +2,7 @@
 import jax.numpy as jnp
 from jax import lax
 from jax.sharding import PartitionSpec as P
+from jax.lax import all_gather
 
 TIME_SPACING = 4
 SHOT_SPACING = 2
@@ -81,7 +82,7 @@
 
 def pseudo_planes(current, observed, shot_delays):
     own = late_shift(current[0], shot_delays[0])
-    blend = lax.psum(own, "vessel").astype(jnp.float32)
+    blend = jnp.sum(all_gather(own, "vessel"), axis=0).astype(jnp.float32)
     resid = observed.astype(jnp.float32) - blend
     plane = current[0].astype(jnp.float32) + early_shift(resid, shot_delays[0])
     return plane.astype(jnp.bfloat16)[None]

time: 137 us -> 87.9 us (0.64)
  waiting for transfers between devices: 49.5 us -> 13.6 us
  between operations: 14.3 us -> 0.92 us
  blocking collectives: 20.2 us -> 24.2 us
  starting transfers between devices: 13.8 us -> 11.8 us
    psum x2 -> x0, waiting for transfers between devices: 35.9 us -> none  [pseudo_planes(): blend = lax.psum(own, 'vessel').astype(jnp.float32)]
    all_gather x0 -> x2, blocking collectives: none -> 3.93 us  [pseudo_planes(): blend = jnp.sum(all_gather(own, 'vessel'), axis=0).astype(jnp.float32)]
    all_to_all x2, starting transfers between devices: 13.8 us -> 11.8 us  [per_device(): lax.all_to_all(planes, 'gather', split_axis=2, concat_axis=1, tiled=True)[0]]
    sub x2, other arithmetic: 1.71 us -> 0.03 us  [pseudo_planes(): resid = observed.astype(jnp.float32) - blend]
    unnamed x26 -> x25, local copies, waits for them, and re-layouts: 5.08 us -> 5.87 us
  transfers between devices with their start and end apart: 4 -> 2, of which waited for: 4 -> 2; matrix products, arithmetic and copies ran while one was open for 0% -> 0% of each run, Pallas kernels for 0% -> 0%
where the time goes in v1:
time: 87.9 us; the launch traced here: 87.3 us
  blocking collectives  24.2 us (28%)
  other arithmetic  22.5 us (26%)
  local copies, waits for them, and re-layouts  13.7 us (16%)
  waiting for transfers between devices  13.6 us (15%)
  starting transfers between devices  11.8 us (13%)
  between operations  0.92 us (1%)
    all_to_all x2, blocking collectives, per_device(): lax.all_to_all(filtered, 'gather', split_axis=1, concat_axis=2, tiled=True)  20.2 us
    all_to_all x2, waiting for transfers between devices, per_device(): lax.all_to_all(planes, 'gather', split_axis=2, concat_axis=1, tiled=True)[0]  13.6 us
    all_to_all x2, starting transfers between devices, per_device(): lax.all_to_all(planes, 'gather', split_axis=2, concat_axis=1, tiled=True)[0]  11.8 us
    reduce_sum x8, other arithmetic, channel(): return (carry + jnp.sum(back, axis=0), None)  7.3 us
    unnamed x25, local copies, waits for them, and re-layouts  5.87 us
    unnamed x8, other arithmetic  4.49 us
    sub x8, other arithmetic, channel(): shrunk = forward_pass - jnp.clip(forward_pass, -bound, bound)  4.06 us
    all_gather x2, blocking collectives, pseudo_planes(): blend = jnp.sum(all_gather(own, 'vessel'), axis=0).astype(jnp.float32)  3.93 us
  transfers between devices with their start and end apart: 2, of which 2 were waited for; matrix products, arithmetic and copies ran while one was open for 0% of the time, Pallas kernels for 0%

profile of v1, /device:TPU:0, one launch (start us, length us, event | category | flops | bytes accessed | tf_op | source)
XLA Modules:
  0.0 87.3 jit_solution(6357473869587097281)
XLA Ops:
  0.7 0.9 %pad_dynamic-slice_fusion.3 = bf16[1,16,2048]{2,1,0:T(8,128)(2,1)S(1)} fusion(s32[]{:T(128)} %bitcast.5, bf16[1,16,2048]{2,1,0:T(8,128)(2,1)} %bitcast.123), kind=kLoop, calls=%fused_computation.151 | loop fusion | bytes 131076 | tf_op jit(solution)/shard_map/vmap()/gather | solution.py:18
  1.6 2.0 %all-gather = bf16[2,16,2048]{2,1,0:T(8,128)(2,1)S(1)} all-gather(bf16[1,16,2048]{2,1,0:T(8,128)(2,1)S(1)} %pad_dynamic-slice_fusion.3), channel_id=2, replica_groups=mesh['vessel'=2,'gather'=16] {'vessel'}, dimensions={0}, use_global_device_ids=true | all-gather | bytes 196608 | tf_op jit(solution)/shard_map/all_gather | solution.py:85
  3.7 0.8 copy-done.1
  4.6 0.7 copy-done
  5.5 0.6 broadcast.734
  6.1 1.0 %reduce.72 = bf16[16,2048]{1,0:T(8,128)(2,1)S(1)} reduce(bf16[16,1,1,2048]{3,2,1,0:T(2,128)(2,1)S(1)} %fusion.64, bf16[]{:T(256)} %broadcast.734), dimensions={1,2}, to_apply=%fusion.64.reduce_sub_computation | reduce | bytes 131074
  7.1 0.7 reshape.661
  7.8 8.3 %all-to-all-start = ((bf16[16,2,1024]{2,1,0:T(2,128)(2,1)}), bf16[16,2,1024]{2,1,0:T(2,128)(2,1)S(1)}, u32[]{:S(2)}, u32[]{:S(2)}) async-start(bf16[16,2,1024]{2,1,0:T(2,128)(2,1)} %reshape.661), calls=%async_computation | async-start | bytes 131072 | tf_op jit(solution)/shard_map/all_to_all | solution.py:98
  16.2 0.6 copy-done.3
  16.9 0.6 copy-done.4
  17.6 6.1 %all-to-all-done = bf16[16,2,1024]{2,1,0:T(2,128)(2,1)S(1)} async-done(((bf16[16,2,1024]{2,1,0:T(2,128)(2,1)}), bf16[16,2,1024]{2,1,0:T(2,128)(2,1)S(1)}, u32[]{:S(2)}, u32[]{:S(2)}) %all-to-all-start) | async-done | bytes 65568 | tf_op jit(solution)/shard_map/all_to_all | solution.py:98
  23.9 12.3 %while.30 = (s32[]{:T(128)}, f32[16,1,2048]{2,0,1:T(8,128)S(1)}, f32[4,4,7]{2,1,0:T(4,128)S(1)}, f32[4,4,7]{2,1,0:T(4,128)S(1)}, f32[1,16,1,2048]{3,1,2,0:T(8,12...) while((s32[]{:T(128)}, f32[16,1,2048]{2,0,1:T(8,128)S(1)}, f32[4,4,7]{2,1,0:T(4,128)S(1)}, ...), condition=%wide.region_3.4_spmd.clone, body=%wide.region_1.3_spmd.clone.sunk | while | flops 7372807 | bytes 5506551 | solution.py:77
  24.2 0.3 slice_bitcast_fusion.14
  24.5 0.3 multiply_add_fusion.4
  24.8 0.3 slice_reduce_fusion.33
  25.0 0.5 minimum_subtract_fusion.4
  25.6 0.4 fusion.71
  26.0 0.9 %add_reduce_fusion.4 = f32[16,2048]{1,0:T(8,128)S(1)} fusion(f32[4,16,1,2048]{3,1,2,0:T(8,128)S(1)} %fusion.71, f32[4]{0:T(128)S(1)} %get-tuple-element.497, f32[4]{0:T(128)S(1)} %get-tuple-element.499, f32[4]{0:T(128)S(1)} %get-tuple-element.501, f32[4]{0:T(128)S(1)} %get-tuple-element.502, f32[4]{0:T(128)S(1)} %get-tuple-element.504, ...), kind=kLoop, calls=%fused_computation.36.clone.1 | loop fusion | flops 1802240 | bytes 655472 | tf_op jit(solution)/shard_map/while/body/eval_jaxpr/reduce_sum | solution.py:75
  27.3 0.3 slice_bitcast_fusion.14
  27.5 0.3 multiply_add_fusion.4
  28.1 0.5 minimum_subtract_fusion.4
  28.6 0.4 fusion.71
  29.1 0.9 %add_reduce_fusion.4 = f32[16,2048]{1,0:T(8,128)S(1)} fusion(f32[4,16,1,2048]{3,1,2,0:T(8,128)S(1)} %fusion.71, f32[4]{0:T(128)S(1)} %get-tuple-element.497, f32[4]{0:T(128)S(1)} %get-tuple-element.499, f32[4]{0:T(128)S(1)} %get-tuple-element.501, f32[4]{0:T(128)S(1)} %get-tuple-element.502, f32[4]{0:T(128)S(1)} %get-tuple-element.504, ...), kind=kLoop, calls=%fused_computation.36.clone.1 | loop fusion | flops 1802240 | bytes 655472 | tf_op jit(solution)/shard_map/while/body/eval_jaxpr/reduce_sum | solution.py:75
  30.3 0.3 slice_bitcast_fusion.14
  30.6 0.3 multiply_add_fusion.4
  31.2 0.5 minimum_subtract_fusion.4
  31.7 0.4 fusion.71
  32.1 0.9 %add_reduce_fusion.4 = f32[16,2048]{1,0:T(8,128)S(1)} fusion(f32[4,16,1,2048]{3,1,2,0:T(8,128)S(1)} %fusion.71, f32[4]{0:T(128)S(1)} %get-tuple-element.497, f32[4]{0:T(128)S(1)} %get-tuple-element.499, f32[4]{0:T(128)S(1)} %get-tuple-element.501, f32[4]{0:T(128)S(1)} %get-tuple-element.502, f32[4]{0:T(128)S(1)} %get-tuple-element.504, ...), kind=kLoop, calls=%fused_computation.36.clone.1 | loop fusion | flops 1802240 | bytes 655472 | tf_op jit(solution)/shard_map/while/body/eval_jaxpr/reduce_sum | solution.py:75
  33.4 0.3 slice_bitcast_fusion.14
  33.7 0.3 multiply_add_fusion.4
  34.2 0.5 minimum_subtract_fusion.4
  34.8 0.4 fusion.71
  35.2 0.9 %add_reduce_fusion.4 = f32[16,2048]{1,0:T(8,128)S(1)} fusion(f32[4,16,1,2048]{3,1,2,0:T(8,128)S(1)} %fusion.71, f32[4]{0:T(128)S(1)} %get-tuple-element.497, f32[4]{0:T(128)S(1)} %get-tuple-element.499, f32[4]{0:T(128)S(1)} %get-tuple-element.501, f32[4]{0:T(128)S(1)} %get-tuple-element.502, f32[4]{0:T(128)S(1)} %get-tuple-element.504, ...), kind=kLoop, calls=%fused_computation.36.clone.1 | loop fusion | flops 1802240 | bytes 655472 | tf_op jit(solution)/shard_map/while/body/eval_jaxpr/reduce_sum | solution.py:75
  36.3 1.0 %reduce.73 = bf16[16,2048]{1,0:T(8,128)(2,1)S(1)} reduce(bf16[16,1,1,2048]{3,2,1,0:T(2,128)(2,1)S(1)} %bitcast.121, bf16[]{:T(256)} %broadcast.734), dimensions={1,2}, to_apply=%bitcast.100.reduce_sub_computation | reduce | bytes 131074
  37.4 10.1 %all_to_all.19 = bf16[16,2,1024]{2,1,0:T(2,128)(2,1)S(1)} all-to-all(bf16[16,2,1024]{2,1,0:T(2,128)(2,1)S(1)} %reshape.663), channel_id=1, replica_groups=mesh['vessel'=2,'gather'=16] {'gather'}, dimensions={0} | all-to-all | bytes 131072 | tf_op jit(solution)/shard_map/all_to_all | solution.py:105
  47.7 1.9 %all-gather.1 = bf16[2,16,2048]{2,1,0:T(8,128)(2,1)S(1)} all-gather(bf16[1,16,2048]{2,1,0:T(8,128)(2,1)S(1)} %pad_dynamic-slice_fusion.2), channel_id=3, replica_groups=mesh['vessel'=2,'gather'=16] {'vessel'}, dimensions={0}, use_global_device_ids=true | all-gather | bytes 196608 | tf_op jit(solution)/shard_map/all_gather | solution.py:85
  50.0 1.0 %reduce.74 = bf16[16,2048]{1,0:T(8,128)(2,1)S(1)} reduce(bf16[16,1,1,2048]{3,2,1,0:T(2,128)(2,1)S(1)} %fusion.65, bf16[]{:T(256)} %broadcast.734), dimensions={1,2}, to_apply=%fusion.65.reduce_sub_computation | reduce | bytes 131074
  51.0 0.7 reshape.665
  51.7 3.5 %all-to-all-start.2 = ((bf16[16,2,1024]{2,1,0:T(2,128)(2,1)}), bf16[16,2,1024]{2,1,0:T(2,128)(2,1)S(1)}, u32[]{:S(2)}, u32[]{:S(2)}) async-start(bf16[16,2,1024]{2,1,0:T(2,128)(2,1)} %reshape.665), calls=%async_computation.2 | async-start | bytes 131072 | tf_op jit(solution)/shard_map/all_to_all | solution.py:98
  55.2 7.5 %all-to-all-done.2 = bf16[16,2,1024]{2,1,0:T(2,128)(2,1)S(1)} async-done(((bf16[16,2,1024]{2,1,0:T(2,128)(2,1)}), bf16[16,2,1024]{2,1,0:T(2,128)(2,1)S(1)}, u32[]{:S(2)}, u32[]{:S(2)}) %all-to-all-start.2) | async-done | bytes 65568 | tf_op jit(solution)/shard_map/all_to_all | solution.py:98
  63.0 12.3 %while.31 = (s32[]{:T(128)}, f32[16,1,2048]{2,0,1:T(8,128)S(1)}, f32[4,4,7]{2,1,0:T(4,128)S(1)}, f32[4,4,7]{2,1,0:T(4,128)S(1)}, f32[1,16,1,2048]{3,1,2,0:T(8,12...) while((s32[]{:T(128)}, f32[16,1,2048]{2,0,1:T(8,128)S(1)}, f32[4,4,7]{2,1,0:T(4,128)S(1)}, ...), condition=%wide.region_7.8_spmd.clone, body=%wide.region_5.7_spmd.clone.sunk | while | flops 7372807 | bytes 5506551 | solution.py:77
  63.2 0.3 slice_bitcast_fusion.15
  63.5 0.3 multiply_add_fusion.5
  64.1 0.5 minimum_subtract_fusion.5
  64.6 0.4 fusion.73
  65.0 0.9 %add_reduce_fusion.5 = f32[16,2048]{1,0:T(8,128)S(1)} fusion(f32[4,16,1,2048]{3,1,2,0:T(8,128)S(1)} %fusion.73, f32[4]{0:T(128)S(1)} %get-tuple-element.527, f32[4]{0:T(128)S(1)} %get-tuple-element.529, f32[4]{0:T(128)S(1)} %get-tuple-element.531, f32[4]{0:T(128)S(1)} %get-tuple-element.532, f32[4]{0:T(128)S(1)} %get-tuple-element.534, ...), kind=kLoop, calls=%fused_computation.105.clone.1 | loop fusion | flops 1802240 | bytes 655472 | tf_op jit(solution)/shard_map/while/body/eval_jaxpr/reduce_sum | solution.py:75
  66.3 0.3 slice_bitcast_fusion.15
  66.6 0.3 multiply_add_fusion.5
  67.2 0.5 minimum_subtract_fusion.5
  67.7 0.4 fusion.73
  68.1 0.9 %add_reduce_fusion.5 = f32[16,2048]{1,0:T(8,128)S(1)} fusion(f32[4,16,1,2048]{3,1,2,0:T(8,128)S(1)} %fusion.73, f32[4]{0:T(128)S(1)} %get-tuple-element.527, f32[4]{0:T(128)S(1)} %get-tuple-element.529, f32[4]{0:T(128)S(1)} %get-tuple-element.531, f32[4]{0:T(128)S(1)} %get-tuple-element.532, f32[4]{0:T(128)S(1)} %get-tuple-element.534, ...), kind=kLoop, calls=%fused_computation.105.clone.1 | loop fusion | flops 1802240 | bytes 655472 | tf_op jit(solution)/shard_map/while/body/eval_jaxpr/reduce_sum | solution.py:75
  69.4 0.3 slice_bitcast_fusion.15
  69.6 0.3 multiply_add_fusion.5
  70.2 0.5 minimum_subtract_fusion.5
  70.7 0.4 fusion.73
  71.2 0.9 %add_reduce_fusion.5 = f32[16,2048]{1,0:T(8,128)S(1)} fusion(f32[4,16,1,2048]{3,1,2,0:T(8,128)S(1)} %fusion.73, f32[4]{0:T(128)S(1)} %get-tuple-element.527, f32[4]{0:T(128)S(1)} %get-tuple-element.529, f32[4]{0:T(128)S(1)} %get-tuple-element.531, f32[4]{0:T(128)S(1)} %get-tuple-element.532, f32[4]{0:T(128)S(1)} %get-tuple-element.534, ...), kind=kLoop, calls=%fused_computation.105.clone.1 | loop fusion | flops 1802240 | bytes 655472 | tf_op jit(solution)/shard_map/while/body/eval_jaxpr/reduce_sum | solution.py:75
  72.4 0.3 slice_bitcast_fusion.15
  72.7 0.3 multiply_add_fusion.5
  73.3 0.5 minimum_subtract_fusion.5
  73.8 0.4 fusion.73
  74.2 0.9 %add_reduce_fusion.5 = f32[16,2048]{1,0:T(8,128)S(1)} fusion(f32[4,16,1,2048]{3,1,2,0:T(8,128)S(1)} %fusion.73, f32[4]{0:T(128)S(1)} %get-tuple-element.527, f32[4]{0:T(128)S(1)} %get-tuple-element.529, f32[4]{0:T(128)S(1)} %get-tuple-element.531, f32[4]{0:T(128)S(1)} %get-tuple-element.532, f32[4]{0:T(128)S(1)} %get-tuple-element.534, ...), kind=kLoop, calls=%fused_computation.105.clone.1 | loop fusion | flops 1802240 | bytes 655472 | tf_op jit(solution)/shard_map/while/body/eval_jaxpr/reduce_sum | solution.py:75
  75.4 1.0 %reduce.75 = bf16[16,2048]{1,0:T(8,128)(2,1)S(1)} reduce(bf16[16,1,1,2048]{3,2,1,0:T(2,128)(2,1)S(1)} %bitcast.120, bf16[]{:T(256)} %broadcast.734), dimensions={1,2}, to_apply=%bitcast.99.reduce_sub_computation | reduce | bytes 131074
  76.4 10.1 %all_to_all.40 = bf16[16,2,1024]{2,1,0:T(2,128)(2,1)S(1)} all-to-all(bf16[16,2,1024]{2,1,0:T(2,128)(2,1)S(1)} %reshape.667), channel_id=1, replica_groups=mesh['vessel'=2,'gather'=16] {'gather'}, dimensions={0} | all-to-all | bytes 131072 | tf_op jit(solution)/shard_map/all_to_all | solution.py:105
  86.6 0.7 copy.74
  (74 shorter events, 6.2 us)
Async XLA Ops:
  3.6 0.8 copy-start.1
  4.5 0.8 copy-start
  7.8 8.3 %copy-start.2 = (f32[16,7]{0,1:T(8,128)S(1)}, f32[16,7]{0,1:T(8,128)}, u32[]{:S(2)}) copy-start(f32[16,7]{0,1:T(8,128)} %param.13) | copy-start | bytes 1348
  7.8 15.9 %all-to-all-start = ((bf16[16,2,1024]{2,1,0:T(2,128)(2,1)}), bf16[16,2,1024]{2,1,0:T(2,128)(2,1)S(1)}, u32[]{:S(2)}, u32[]{:S(2)}) async-start(bf16[16,2,1024]{2,1,0:T(2,128)(2,1)} %reshape.661), calls=%async_computation | async-start | bytes 131072 | tf_op jit(solution)/shard_map/all_to_all | solution.py:98
  16.1 0.7 copy-start.3
  16.8 0.7 copy-start.4
  51.7 11.0 %all-to-all-start.2 = ((bf16[16,2,1024]{2,1,0:T(2,128)(2,1)}), bf16[16,2,1024]{2,1,0:T(2,128)(2,1)S(1)}, u32[]{:S(2)}, u32[]{:S(2)}) async-start(bf16[16,2,1024]{2,1,0:T(2,128)(2,1)} %reshape.665), calls=%async_computation.2 | async-start | bytes 131072 | tf_op jit(solution)/shard_map/all_to_all | solution.py:98
